TPU v7x, 256 devices: a whole 4x4x8 slice. The times are simulated.
256 devices in a mesh: row: 32 (over z, y), col: 8 (over x, core).
Axes of the slice: x: 4, y: 4, z: 8, core: 2. Of those that a mesh axis runs over, the one named last changes fastest.
Arguments:
- embeddings: bfloat16 [262144, 1024], P('row', 'col'), may hold values from -0.1875 to 0.1875
- quality: float32 [262144], P('row'), may hold values from 0.5 to 2
- probes: float32 [32, 262144], P(None, 'row'), may hold values from -6 to 6
- neighbors: int32 [2048, 8], P('row'), may hold values from 0 to 2047, as said below
Outputs:
- first: float32 [32, 262144], P(None, 'row')
- second: float32 [32, 262144], P(None, 'row')
Inputs may be any that keep to these rules, and one draw needn't show every extreme that they name: `neighbors`: block b is held by row index b // 64. Among the 512 entries of one row index's blocks, at most 8 name blocks of any one other row index, and on every row index some other index is named exactly 8 times; the remaining entries name the index's own blocks.
All inputs are finite; a program needn't handle non-finite values.
Results may differ from a plain program's by a relative error of at most 0.02.
Values may be sent and summed in bfloat16 or wider, within the bound.
A program may use at most 64 MiB of HBM per device.

v0:
```python
import jax
import jax.numpy as jnp
from jax import lax
from jax.sharding import PartitionSpec as P


def body(embeddings, quality, probes, neighbors):
    nrow = lax.axis_size("row")
    myself = lax.axis_index("row")
    blk_count, list_len = neighbors.shape
    docs, width = embeddings.shape
    block_len = docs // blk_count
    nprobe = probes.shape[0]
    slots = max(2, blk_count * list_len // (2 * nrow))
    blocked = embeddings.reshape(blk_count, block_len, width)
    flat = neighbors.reshape(-1)
    owner = flat // blk_count
    local = flat % blk_count
    remote = owner != myself
    onehot = (owner[:, None] == jnp.arange(nrow, dtype=jnp.int32)[None, :]).astype(jnp.int32)
    slot = jnp.sum((jnp.cumsum(onehot, axis=0) - onehot) * onehot, axis=1)
    request = jnp.zeros((nrow, slots), jnp.int32)
    request = request.at[jnp.where(remote, owner, nrow), slot].set(local, mode="drop")
    wanted = lax.all_to_all(request, "row", split_axis=0, concat_axis=0, tiled=True)
    source = jnp.where(remote, blk_count + owner * slots + slot, local)

    def apply(vec):
        scaled = (vec * quality[None, :]).astype(jnp.bfloat16).reshape(nprobe, blk_count, block_len)
        own = jnp.einsum(
            "bdc,pbd->bcp", blocked, scaled, preferred_element_type=jnp.float32
        ).astype(jnp.bfloat16)
        outgoing = own.reshape(blk_count, width * nprobe)[wanted]
        arrived = lax.all_to_all(outgoing, "row", split_axis=0, concat_axis=0, tiled=True)
        table = jnp.concatenate([own, arrived.reshape(nrow * slots, width, nprobe)], axis=0)
        gathered = table[source].reshape(blk_count, list_len, width, nprobe)
        summed = jnp.sum(gathered, axis=1, dtype=jnp.float32).astype(jnp.bfloat16)
        partial_value = jnp.einsum(
            "bdc,bcp->pbd", blocked, summed, preferred_element_type=jnp.float32
        ).reshape(nprobe, docs)
        total = lax.psum(partial_value.astype(jnp.bfloat16), "col").astype(jnp.float32)
        return total * quality[None, :] - vec

    first = apply(probes)
    second = 2.0 * apply(first) - probes
    return (first, second)


def solution(mesh):
    placed = (P("row", "col"), P("row"), P(None, "row"), P("row", None))
    return jax.shard_map(
        body,
        mesh=mesh,
        in_specs=placed,
        out_specs=(P(None, "row"), P(None, "row")),
        check_vma=False,
    )
```

profile of v0, /device:TPU:1, one launch (start us, length us, event | category | flops | bytes accessed | tf_op | source)
XLA Modules:
  0.0 379.7 jit_solution(4146133513576657002)
XLA Ops:
  7.2 0.9 copy.27
  8.4 1.2 reduce-window.6
  10.1 22.3 %scatter_fusion = s32[32,8]{0,1:T(8,128)S(1)} fusion(s32[32,8]{0,1:T(8,128)S(1)} %broadcast.250, s32[512]{0:T(512)S(1)} %bitcast.75, s32[512]{0:T(512)S(1)} %get-tuple-element.6), kind=kCustom, calls=%fused_computation.4 | custom fusion | bytes 10240 | tf_op jit(solution)/shard_map/scatter | solution.py:23
  33.0 12.0 %all-to-all-start = ((s32[32,1,8]{2,1,0:T(1,128)}), s32[32,1,8]{2,1,0:T(1,128)S(1)}, u32[]{:S(2)}, u32[]{:S(2)}) async-start(s32[32,1,8]{2,1,0:T(1,128)} %copy.31), calls=%async_computation | async-start | bytes 32768 | tf_op jit(solution)/shard_map/all_to_all | solution.py:24
  45.1 1.5 fusion
  46.5 3.7 copy.26
  50.2 1.5 copy.32
  51.8 1.9 all-to-all-done
  53.8 3.2 gather_fusion
  57.0 7.5 %all-to-all-start.1 = ((bf16[32,8,4096]{2,1,0:T(8,128)(2,1)}), bf16[32,8,4096]{2,1,0:T(8,128)(2,1)}, u32[]{:S(2)}, u32[]{:S(2)}) async-start(bf16[32,8,4096]{2,1,0:T(8,128)(2,1)} %bitcast.76), calls=%async_computation.1 | async-start | bytes 4194304 | tf_op jit(solution)/shard_map/all_to_all | solution.py:33
  64.5 47.9 %all-to-all-done.1 = bf16[32,8,4096]{2,1,0:T(8,128)(2,1)} async-done(((bf16[32,8,4096]{2,1,0:T(8,128)(2,1)}), bf16[32,8,4096]{2,1,0:T(8,128)(2,1)}, u32[]{:S(2)}, u32[]{:S(2)}) %all-to-all-start.1) | async-done | bytes 2097184 | tf_op jit(solution)/shard_map/all_to_all | solution.py:33
  112.4 9.4 %reshape.270 = bf16[256,128,32]{2,1,0:T(8,128)(2,1)} reshape(bf16[32,8,4096]{2,1,0:T(8,128)(2,1)} %all-to-all-done.1) | data formatting | bytes 4194304 | tf_op jit(solution)/shard_map/reshape | solution.py:34
  121.8 8.0 %copy.33 = bf16[256,128,32]{1,2,0:T(8,128)(2,1)} copy(bf16[256,128,32]{2,1,0:T(8,128)(2,1)} %reshape.270) | data formatting | bytes 4194304 | tf_op jit(solution)/shard_map/reshape | solution.py:34
  129.7 3.3 pad_maximum_fusion
  133.1 4.9 %gather_fusion.1 = bf16[512,128,32]{1,2,0:T(8,128)(2,1)} fusion(bf16[320,128,32]{1,2,0:T(8,128)(2,1)} %pad_maximum_fusion, s32[1024]{0:T(1024)S(1)} %pad_clamp_fusion), kind=kCustom, calls=%fused_computation.1 | custom fusion | bytes 8390656 | tf_op jit(solution)/shard_map/gather | solution.py:35
  138.0 3.1 bitcast_reduce_fusion.1
  141.1 1.2 fusion.1
  142.3 0.9 copy.65
  143.4 63.8 %all-reduce.3.cloned.1.call-done = bf16[32,8192]{1,0:T(8,128)(2,1)} async-done(((bf16[32,8192]{1,0:T(8,128)(2,1)}), bf16[32,8192]{1,0:T(8,128)(2,1)}) %all-reduce.3.cloned.1.call-update) | async-done | bytes 524304 | tf_op jit(solution)/shard_map/psum | solution.py:40
  207.2 2.2 fusion.5
  210.1 2.6 copy.38
  212.7 1.5 copy.39
  214.3 3.2 gather_fusion.2
  217.5 57.1 %all_to_all.22 = bf16[32,8,4096]{2,1,0:T(8,128)(2,1)} all-to-all(bf16[32,8,4096]{2,1,0:T(8,128)(2,1)} %bitcast.77), channel_id=1, replica_groups=mesh['row'=32,'col'=8] {'row'}, dimensions={0} | all-to-all | bytes 4194304 | tf_op jit(solution)/shard_map/all_to_all | solution.py:33
  274.6 9.4 %reshape.274 = bf16[256,128,32]{2,1,0:T(8,128)(2,1)} reshape(bf16[32,8,4096]{2,1,0:T(8,128)(2,1)} %all_to_all.22) | data formatting | bytes 4194304 | tf_op jit(solution)/shard_map/reshape | solution.py:34
  283.9 7.9 %copy.40 = bf16[256,128,32]{1,2,0:T(8,128)(2,1)} copy(bf16[256,128,32]{2,1,0:T(8,128)(2,1)} %reshape.274) | data formatting | bytes 4194304 | tf_op jit(solution)/shard_map/reshape | solution.py:34
  291.8 3.3 pad_maximum_fusion.1
  295.2 4.9 %gather_fusion.3 = bf16[512,128,32]{1,2,0:T(8,128)(2,1)} fusion(bf16[320,128,32]{1,2,0:T(8,128)(2,1)} %pad_maximum_fusion.1, s32[1024]{0:T(1024)S(1)} %pad_clamp_fusion), kind=kCustom, calls=%fused_computation.3 | custom fusion | bytes 8390656 | tf_op jit(solution)/shard_map/gather | solution.py:35
  300.0 3.1 bitcast_reduce_fusion
  303.2 1.2 fusion.3
  305.3 65.0 %all-reduce.5.cloned.1.call-done = bf16[32,8192]{1,0:T(8,128)(2,1)} async-done(((bf16[32,8192]{1,0:T(8,128)(2,1)}), bf16[32,8192]{1,0:T(8,128)(2,1)}) %all-reduce.5.cloned.1.call-update) | async-done | bytes 524304 | tf_op jit(solution)/shard_map/psum | solution.py:40
  370.4 2.5 multiply_subtract_fusion
  (36 shorter events, 3.4 us)
Async XLA Ops:
  7.2 37.9 %copy-start = (bf16[8192,128]{1,0:T(8,128)(2,1)S(1)}, bf16[8192,128]{1,0:T(8,128)(2,1)}, u32[]{:S(2)}) copy-start(bf16[8192,128]{1,0:T(8,128)(2,1)} %param.4) | copy-start | bytes 6291460
  10.0 35.0 %copy-start.1 = (f32[32,8192]{1,0:T(8,128)S(1)}, f32[32,8192]{1,0:T(8,128)}, u32[]{:S(2)}) copy-start(f32[32,8192]{1,0:T(8,128)} %param.6) | copy-start | bytes 3145732
  10.1 35.0 %copy-start.5 = (f32[8192]{0:T(1024)S(1)}, f32[8192]{0:T(1024)}, u32[]{:S(2)}) copy-start(f32[8192]{0:T(1024)} %param.5) | copy-start | bytes 98308
  33.0 20.7 %all-to-all-start = ((s32[32,1,8]{2,1,0:T(1,128)}), s32[32,1,8]{2,1,0:T(1,128)S(1)}, u32[]{:S(2)}, u32[]{:S(2)}) async-start(s32[32,1,8]{2,1,0:T(1,128)} %copy.31), calls=%async_computation | async-start | bytes 32768 | tf_op jit(solution)/shard_map/all_to_all | solution.py:24
  57.0 55.4 %all-to-all-start.1 = ((bf16[32,8,4096]{2,1,0:T(8,128)(2,1)}), bf16[32,8,4096]{2,1,0:T(8,128)(2,1)}, u32[]{:S(2)}, u32[]{:S(2)}) async-start(bf16[32,8,4096]{2,1,0:T(8,128)(2,1)} %bitcast.76), calls=%async_computation.1 | async-start | bytes 4194304 | tf_op jit(solution)/shard_map/all_to_all | solution.py:33
  64.5 142.8 %all-reduce.3.cloned.1.call-start = ((), (), s32[]{:S(2)}) async-start(), calls=%async_computation.3 | async-start | bytes 1048576 | tf_op jit(solution)/shard_map/psum | solution.py:40
  121.8 8.0 %copy-start.4 = (bf16[64,128,32]{1,2,0:T(8,128)(2,1)S(1)}, bf16[64,128,32]{1,2,0:T(8,128)(2,1)}, u32[]{:S(2)}) copy-start(bf16[64,128,32]{1,2,0:T(8,128)(2,1)} %fusion) | copy-start | bytes 1572868
  141.1 66.2 %copy-start.2 = (f32[32,8192]{1,0:T(8,128)S(1)}, f32[32,8192]{1,0:T(8,128)}, u32[]{:S(2)}) copy-start(f32[32,8192]{1,0:T(8,128)} %param.6) | copy-start | bytes 3145732
  143.2 227.1 %all-reduce.5.cloned.1.call-start = ((), (), s32[]{:S(2)}) async-start(), calls=%async_computation.4 | async-start | bytes 1048576 | tf_op jit(solution)/shard_map/psum | solution.py:40
  303.2 67.2 %copy-start.3 = (f32[32,8192]{1,0:T(8,128)S(1)}, f32[32,8192]{1,0:T(8,128)}, u32[]{:S(2)}) copy-start(f32[32,8192]{1,0:T(8,128)} %param.6) | copy-start | bytes 3145732
Sparse Core Ops, SparseCore 0:
  143.3 63.8 all-reduce.2
  305.4 64.8 all-reduce.4
where the time goes:
time: 382 us; the launch traced here: 380 us
  waiting for transfers between devices  179 us (47%)
  local copies, waits for them, and re-layouts  86.4 us (23%)
  blocking collectives  57.1 us (15%)
  starting transfers between devices  19.8 us (5%)
  other arithmetic  19 us (5%)
  between operations  14.2 us (4%)
  matrix products  4.49 us (1%)
    psum x2, waiting for transfers between devices, apply(): lax.psum(partial_value.astype(jnp.bfloat16), 'col').astype(jnp.float32)  129 us
    all_to_all x1, blocking collectives, apply(): lax.all_to_all(outgoing, 'row', split_axis=0, concat_axis=0, tiled=True)  57.1 us
    all_to_all x1, waiting for transfers between devices, apply(): lax.all_to_all(outgoing, 'row', split_axis=0, concat_axis=0, tiled=True)  47.9 us
    reshape x4, local copies, waits for them, and re-layouts, apply(): arrived.reshape(nrow * slots, width, nprobe)  34.6 us
    scatter x1, local copies, waits for them, and re-layouts, body(): request.at[jnp.where(remote, owner, nrow), slot].set(local, mode='drop')  22.3 us
    all_to_all x1, starting transfers between devices, body(): lax.all_to_all(request, 'row', split_axis=0, concat_axis=0, tiled=True)  12 us
    gather x2, local copies, waits for them, and re-layouts, apply(): gathered = table[source].reshape(blk_count, list_len, width, nprobe)  9.75 us
    unnamed x3, other arithmetic  8.43 us
  transfers between devices with their start and end apart: 4, of which 4 were waited for; matrix products, arithmetic and copies ran while one was open for 2% of the time, Pallas kernels for 0%

commit v1 on v0

v1 whole, which is shorter than its diff:
```python
import functools

import jax
import jax.numpy as jnp
from jax import lax
from jax.experimental import pallas as pl
from jax.experimental.pallas import tpu as pltpu
from jax.sharding import PartitionSpec as P

MESH = pl.DeviceIdType.MESH
NY = 4
CH = 16
F32 = jnp.float32
BF16 = jnp.bfloat16


def kernel(nz, ny, ncol, blk, knn, nch, idx_ref, req_ref, emb_ref, q_ref, v_ref, first_ref, second_ref, *scratch):
    scratch = list(scratch)
    nset = 2 * nch
    deep = nz // 2
    half = blk // 2
    piece = blk // ncol
    slots = [[scratch.pop(0) for _ in range(nz)] for _ in range(nset)]
    stage = [scratch.pop(0) for _ in range(nset)]
    table = [scratch.pop(0) for _ in range(nset)]
    part = [scratch.pop(0) for _ in range(nset)]
    recv = [scratch.pop(0) for _ in range(nset)]
    mine = [scratch.pop(0) for _ in range(nset)]
    full = [scratch.pop(0) for _ in range(nset)]
    ask_vmem, ask, z_send, z_recv, y_send, y_recv, x_send, x_recv, ask_send, ask_recv, ask_sem = scratch

    row, col = lax.axis_index("row"), lax.axis_index("col")
    z, y = row // ny, row % ny
    up = (lax.rem(z + 1, nz) * ny + y, col)
    down = (lax.rem(z + nz - 1, nz) * ny + y, col)

    def mate(m):
        return (z * ny + lax.rem(y + m, ny), col)

    def peer(r):
        return lax.rem(col + r, ncol)

    barrier = pltpu.get_barrier_semaphore()
    partners = [up, down] + [mate(m) for m in range(1, ny)] + [(row, peer(r)) for r in range(1, ncol)]
    for device in partners:
        pl.semaphore_signal(barrier, inc=1, device_id=device, device_id_type=MESH)
    pl.semaphore_wait(barrier, len(partners))

    def ask_copy(r):
        return pltpu.make_async_remote_copy(
            src_ref=req_ref.at[r], dst_ref=ask_vmem.at[ny - r],
            send_sem=ask_send.at[r], recv_sem=ask_recv.at[ny - r],
            device_id=mate(r), device_id_type=MESH)

    for r in range(1, ny):
        ask_copy(r).start()
    ask_vmem[0] = req_ref[0]

    def block(b):
        return pl.ds(pl.multiple_of(b * 128, 128), 128)

    def rows_of(n):
        return pl.ds((n % nch) * CH, CH)

    def sums(n, b, weights):
        value = jnp.dot(weights, emb_ref[block(b), :], preferred_element_type=F32).astype(BF16)
        slots[n][0][b] = value
        table[n][ny * nz * 8 + b] = value

    def first_sums(n):
        def body(g, carry):
            for i in range(8):
                b = g * 8 + i
                scaled = (v_ref[rows_of(n), block(b)] * q_ref[pl.ds(b, 1), :]).astype(BF16)
                sums(n, b, scaled)
            return carry

        lax.fori_loop(0, blk // 8, body, 0)

    def slot_of(d, upward):
        if d == 0:
            return 0
        return nz - 1 if d == deep else (2 * d - 1 if upward else 2 * d)

    def z_copy(n, d, k, upward):
        h = k if upward else 1 - k
        part_of = pl.ds(h * half, half)
        sem = ((d - 1) * 2 + k) * 2 + int(upward)
        return pltpu.make_async_remote_copy(
            src_ref=slots[n][slot_of(d - 1, upward)].at[part_of],
            dst_ref=slots[n][slot_of(d, upward)].at[part_of],
            send_sem=z_send.at[n, sem], recv_sem=z_recv.at[n, sem],
            device_id=up if upward else down, device_id_type=MESH)

    def z_start(n, d, k):
        if d < deep or (d == deep and k == 0):
            for upward in (True, False):
                z_copy(n, d, k, upward).start()

    def z_wait(n, d, k):
        for upward in (True, False):
            z_copy(n, d, k, upward).wait_recv()

    def group(d):
        if d == 0:
            return (0,)
        return (nz - 1,) if d == deep else (2 * d - 1, 2 * d)

    def y_stage(n, d):
        ps = group(d)

        def body(t, carry):
            for p in ps:
                for m in range(ny):
                    value = slots[n][p][ask[m, 0, p * 8 + t]]
                    if m == 0:
                        table[n][p * 8 + t] = value
                    else:
                        stage[n][((m - 1) * nz + p) * 8 + t] = value
            return carry

        lax.fori_loop(0, 8, body, 0)
        rows = len(ps) * 8
        for m in range(1, ny):
            pltpu.make_async_remote_copy(
                src_ref=stage[n].at[pl.ds(((m - 1) * nz + ps[0]) * 8, rows)],
                dst_ref=table[n].at[pl.ds(((ny - m) * nz + ps[0]) * 8, rows)],
                send_sem=y_send.at[n], recv_sem=y_recv.at[n],
                device_id=mate(m), device_id_type=MESH).start()

    def y_all(n):
        return pltpu.make_async_remote_copy(
            src_ref=stage[n], dst_ref=table[n].at[pl.ds(nz * 8, (ny - 1) * nz * 8)],
            send_sem=y_send.at[n], recv_sem=y_recv.at[n],
            device_id=mate(1), device_id_type=MESH)

    def partial_piece(n, j):
        for i in range(piece):
            b = j * piece + i
            total = table[n][idx_ref[b * knn]].astype(F32)
            for k in range(1, knn):
                total += table[n][idx_ref[b * knn + k]].astype(F32)
            value = lax.dot_general(total.astype(BF16), emb_ref[block(b), :], (((1,), (1,)), ((), ())),
                                    preferred_element_type=F32)
            part[n][b] = value.astype(BF16)

    def scatter_copy(n, r):
        return pltpu.make_async_remote_copy(
            src_ref=part[n].at[pl.ds(peer(r) * piece, piece)],
            dst_ref=recv[n].at[pl.ds((r - 1) * piece, piece)],
            send_sem=x_send.at[n, 0], recv_sem=x_recv.at[n, 0],
            device_id=(row, peer(r)), device_id_type=MESH)

    def scatter_all(n):
        return pltpu.make_async_remote_copy(
            src_ref=part[n].at[pl.ds(0, (ncol - 1) * piece)], dst_ref=recv[n],
            send_sem=x_send.at[n, 0], recv_sem=x_recv.at[n, 0],
            device_id=(row, peer(1)), device_id_type=MESH)

    def gather_copy(n, r):
        return pltpu.make_async_remote_copy(
            src_ref=mine[n], dst_ref=full[n].at[pl.ds(col * piece, piece)],
            send_sem=x_send.at[n, 1], recv_sem=x_recv.at[n, 1],
            device_id=(row, peer(r)), device_id_type=MESH)

    def gather_all(n):
        return pltpu.make_async_remote_copy(
            src_ref=recv[n], dst_ref=full[n].at[pl.ds(0, (ncol - 1) * piece)],
            send_sem=x_send.at[n, 1], recv_sem=x_recv.at[n, 1],
            device_id=(row, peer(1)), device_id_type=MESH)

    def post_a(n):
        y_all(n).wait_recv()

        def body(r, carry):
            partial_piece(n, peer(r))
            scatter_copy(n, r).start()
            return carry

        lax.fori_loop(1, ncol, body, 0)
        partial_piece(n, col)

    def post_b(n):
        scatter_all(n).wait_recv()
        for i in range(piece):
            total = part[n][col * piece + i].astype(F32)
            for r in range(1, ncol):
                total += recv[n][(r - 1) * piece + i].astype(F32)
            total = total.astype(BF16)
            mine[n][i] = total
            full[n][col * piece + i] = total
        for r in range(1, ncol):
            gather_copy(n, r).start()

    def post_c(n):
        gather_all(n).wait_recv()

        def body(g, carry):
            for i in range(8):
                b = g * 8 + i
                quality = q_ref[pl.ds(b, 1), :]
                value = v_ref[rows_of(n), block(b)]
                total = full[n][b].astype(F32) * quality
                if n < nch:
                    first = total - value
                    first_ref[rows_of(n), block(b)] = first
                    sums(n + nch, b, (first * quality).astype(BF16))
                else:
                    second_ref[rows_of(n), block(b)] = 2.0 * (total - first_ref[rows_of(n), block(b)]) - value
            return carry

        lax.fori_loop(0, blk // 8, body, 0)

    def begin(n):
        z_start(n, 1, 0)
        z_start(n, 1, 1)
        y_stage(n, 0)

    first_sums(0)
    z_start(0, 1, 0)
    z_start(0, 1, 1)
    for n in range(1, nch):
        first_sums(n)
    for r in range(1, ny):
        ask_copy(r).wait_recv()
    to_smem = pltpu.make_async_copy(ask_vmem, ask, ask_sem)
    to_smem.start()
    to_smem.wait()
    y_stage(0, 0)

    events = [(d, k) for d in range(1, deep) for k in (0, 1)]
    for n in range(nset):
        posts = {0: post_a, min(2, len(events) - 1): post_b}
        for e, (d, k) in enumerate(events):
            z_wait(n, d, k)
            z_start(n, d + 1, k)
            if k == 1:
                y_stage(n, d)
            if n > 0:
                if e == 0:
                    post_a(n - 1)
                if e == min(2, len(events) - 1):
                    post_b(n - 1)
                if e == min(4, len(events) - 1):
                    post_c(n - 1)
        if n + 1 < nset:
            begin(n + 1)
        z_wait(n, deep, 0)
        y_stage(n, deep)
    post_a(nset - 1)
    post_b(nset - 1)
    post_c(nset - 1)

    for r in range(1, ny):
        ask_copy(r).wait_send()
    for n in range(nset):
        for d in range(1, deep + 1):
            for k in (0, 1):
                if d < deep or k == 0:
                    for upward in (True, False):
                        z_copy(n, d, k, upward).wait_send()
        y_all(n).wait_send()
        scatter_all(n).wait_send()
        gather_all(n).wait_send()


def tables(neighbors, nz, ny):
    blk, knn = neighbors.shape
    row = lax.axis_index("row")
    z, y = row // ny, row % ny
    flat = neighbors.reshape(-1)
    owner, local = flat // blk, flat % blk
    order = jnp.arange(blk * knn, dtype=jnp.int32)
    before = (owner[:, None] == owner[None, :]) & (order[:, None] < order[None, :])
    rank = jnp.sum(before.astype(jnp.int32), axis=0)
    delta = (owner // ny - z + nz) % nz
    r = (owner % ny - y + ny) % ny
    p = jnp.where(delta < nz // 2, 2 * delta, 2 * (nz - delta) - 1)
    key = jnp.where((owner != row) & (rank < 8), (r * nz + p) * 8 + rank, ny * nz * 8)
    index = jnp.where(owner == row, ny * nz * 8 + local, key)
    hit = key[:, None] == jnp.arange(ny * nz * 8, dtype=jnp.int32)[None, :]
    request = jnp.sum(jnp.where(hit, local[:, None], 0), axis=0).reshape(ny, 1, nz * 8)
    request = jnp.pad(request, ((0, 0), (0, 7), (0, 128 - nz * 8)))
    return index, request


def body(embeddings, quality, probes, neighbors, ny=NY, ncol=8, nz=8):
    blk, knn = neighbors.shape
    nch = probes.shape[0] // CH
    nset = 2 * nch
    piece = blk // ncol
    index, request = tables(neighbors, nz, ny)

    def blocks(count):
        return [pltpu.VMEM((count, CH, 128), BF16)] * nset

    vmem = pl.BlockSpec(memory_space=pltpu.VMEM)
    return pl.pallas_call(
        functools.partial(kernel, nz, ny, ncol, blk, knn, nch),
        out_shape=[jax.ShapeDtypeStruct(probes.shape, F32)] * 2,
        in_specs=[pl.BlockSpec(memory_space=pltpu.SMEM), vmem, vmem, vmem, vmem],
        out_specs=[vmem, vmem],
        scratch_shapes=blocks(blk) * nz
        + blocks((ny - 1) * nz * 8)
        + blocks(ny * nz * 8 + blk)
        + blocks(blk)
        + blocks((ncol - 1) * piece)
        + blocks(piece)
        + blocks(blk)
        + [
            pltpu.VMEM((ny, 8, 128), jnp.int32),
            pltpu.SMEM((ny, 8, 128), jnp.int32),
            pltpu.SemaphoreType.DMA((nset, 2 * nz)),
            pltpu.SemaphoreType.DMA((nset, 2 * nz)),
            pltpu.SemaphoreType.DMA((nset,)),
            pltpu.SemaphoreType.DMA((nset,)),
            pltpu.SemaphoreType.DMA((nset, 2)),
            pltpu.SemaphoreType.DMA((nset, 2)),
            pltpu.SemaphoreType.DMA((ny,)),
            pltpu.SemaphoreType.DMA((ny,)),
            pltpu.SemaphoreType.DMA,
        ],
        compiler_params=pltpu.CompilerParams(
            collective_id=0, has_side_effects=True, vmem_limit_bytes=56 * 1024 * 1024),
    )(index, request, embeddings, quality.reshape(blk, 128), probes)


def solution(mesh):
    placed = (P("row", "col"), P("row"), P(None, "row"), P("row", None))
    return jax.shard_map(
        lambda *arrays: tuple(body(*arrays)),
        mesh=mesh,
        in_specs=placed,
        out_specs=(P(None, "row"), P(None, "row")),
        check_vma=False,
    )
```

time: 382 us -> 121 us (0.32)
  waiting for transfers between devices: 179 us -> 0 us
  Pallas kernels: 0 us -> 114 us
  local copies, waits for them, and re-layouts: 86.4 us -> 4.89 us
  blocking collectives: 57.1 us -> 0 us
  starting transfers between devices: 19.8 us -> 0 us
  other arithmetic: 19 us -> 1.02 us
  between operations: 14.2 us -> 0.68 us
  matrix products: 4.49 us -> 0 us
    psum x2 -> x0, waiting for transfers between devices: 129 us -> none  [apply(): lax.psum(partial_value.astype(jnp.bfloat16), 'col').astype(jnp.float32)]
    pallas_call x0 -> x1, Pallas kernels: none -> 114 us  [body(): pl.pallas_call(functools.partial(kernel, nz, ny, ncol, blk, knn, nch), ou...]
    all_to_all x1 -> x0, blocking collectives: 57.1 us -> none  [apply(): lax.all_to_all(outgoing, 'row', split_axis=0, concat_axis=0, tiled=True)]
    all_to_all x2 -> x0, waiting for transfers between devices: 49.8 us -> none  [the longest x1 47.9 us: apply(): lax.all_to_all(outgoing, 'row', split_axis=0, concat_axis=0, tiled=True)]
    reshape x9 -> x2, local copies, waits for them, and re-layouts: 38 us -> 0.18 us  [the longest x1 0.09 us: tables(): flat = neighbors.reshape(-1)]
    scatter x1 -> x0, local copies, waits for them, and re-layouts: 22.3 us -> none  [body(): request.at[jnp.where(remote, owner, nrow), slot].set(local, mode='drop')]
    all_to_all x2 -> x0, starting transfers between devices: 19.5 us -> none  [the longest x1 12 us: body(): lax.all_to_all(request, 'row', split_axis=0, concat_axis=0, tiled=True)]
    gather x4 -> x0, local copies, waits for them, and re-layouts: 16.2 us -> none  [the longest x2 9.75 us: apply(): gathered = table[source].reshape(blk_count, list_len, width, nprobe)]
  transfers between devices with their start and end apart: 4 -> 0, of which waited for: 4 -> 0; matrix products, arithmetic and copies ran while one was open for 2% -> 0% of each run, Pallas kernels for 0% -> 0%
where the time goes in v1:
time: 121 us
  Pallas kernels  114 us (94%)
  local copies, waits for them, and re-layouts  4.89 us (4%)
    pallas_call x1, Pallas kernels, body(): pl.pallas_call(functools.partial(kernel, nz, ny, ncol, blk, knn, nch), ou...  114 us
    unnamed x5, local copies, waits for them, and re-layouts  4.1 us

profile of v1, /device:TPU:1, one launch (start us, length us, event | category | flops | bytes accessed | tf_op | source)
XLA Modules:
  0.0 121.1 jit_solution(3280308536254998247)
XLA Ops:
  0.7 0.8 copy.7
  1.4 0.1 reshape.167
  1.5 0.2 convert_reduce_fusion
  1.7 0.6 add_select_fusion.6
  2.3 0.2 select_reduce_fusion
  2.5 0.1 reshape.168
  2.6 0.6 pad.4.req_ref
  3.2 114.5 %shard_map.59 = (f32[32,8192]{1,0:T(8,128)}, f32[32,8192]{1,0:T(8,128)}) custom-call(s32[512]{0:T(512)} %get-tuple-element.2.idx_ref, s32[4,8,128]{2,1,0:T(8,128)} %pad.4.req_ref, bf16[8192,128]{1,0:T(8,128)(2,1)} %emb_ref.1, f32[64,128]{1,0:T(8,128)} %bitcast.1, f32[32,8192]{1,0:T(8,128)} %v_ref.1), custom_call_target="tpu_custom_call" | custom-call | tf_op jit(solution)/shard_map/pallas_call | solution.py:298
  117.7 0.0 copy-start
  117.7 2.4 %copy.10 = f32[32,8192]{1,0:T(8,128)} copy(f32[32,8192]{1,0:T(8,128)} %get-tuple-element.7) | data formatting | bytes 2097152
  120.1 0.0 copy-done
  120.1 1.0 copy.11
  (1 shorter events, 0.0 us)
Async XLA Ops:
  117.7 2.4 %copy-start = (f32[32,8192]{1,0:T(8,128)S(1)}, f32[32,8192]{1,0:T(8,128)}, u32[]{:S(2)}) copy-start(f32[32,8192]{1,0:T(8,128)} %get-tuple-element.8) | copy-start | bytes 3145732

commit v2 on v1

--- a/solution.py
+++ b/solution.py
@@ -14,7 +14,7 @@
 BF16 = jnp.bfloat16
 
 
-def kernel(nz, ny, ncol, blk, knn, nch, idx_ref, req_ref, emb_ref, q_ref, v_ref, first_ref, second_ref, *scratch):
+def kernel(nz, ny, ncol, blk, knn, nch, idx_ref, req_ref, emb_hbm, q_hbm, v_hbm, total1_ref, total2_ref, *scratch):
     scratch = list(scratch)
     nset = 2 * nch
     deep = nz // 2
@@ -27,7 +27,12 @@
     recv = [scratch.pop(0) for _ in range(nset)]
     mine = [scratch.pop(0) for _ in range(nset)]
     full = [scratch.pop(0) for _ in range(nset)]
-    ask_vmem, ask, z_send, z_recv, y_send, y_recv, x_send, x_recv, ask_send, ask_recv, ask_sem = scratch
+    emb_ref, q_ref, v_ref, load_sem, ask_vmem, ask, z_send, z_recv, y_send, y_recv, x_send, x_recv, ask_send, ask_recv, ask_sem = scratch
+
+    loads = [pltpu.make_async_copy(src, dst, load_sem.at[i])
+             for i, (src, dst) in enumerate(((v_hbm, v_ref), (q_hbm, q_ref), (emb_hbm, emb_ref)))]
+    for load in loads:
+        load.start()
 
     row, col = lax.axis_index("row"), lax.axis_index("col")
     z, y = row // ny, row % ny
@@ -44,7 +49,6 @@
     partners = [up, down] + [mate(m) for m in range(1, ny)] + [(row, peer(r)) for r in range(1, ncol)]
     for device in partners:
         pl.semaphore_signal(barrier, inc=1, device_id=device, device_id_type=MESH)
-    pl.semaphore_wait(barrier, len(partners))
 
     def ask_copy(r):
         return pltpu.make_async_remote_copy(
@@ -52,8 +56,6 @@
             send_sem=ask_send.at[r], recv_sem=ask_recv.at[ny - r],
             device_id=mate(r), device_id_type=MESH)
 
-    for r in range(1, ny):
-        ask_copy(r).start()
     ask_vmem[0] = req_ref[0]
 
     def block(b):
@@ -202,23 +204,22 @@
                 value = v_ref[rows_of(n), block(b)]
                 total = full[n][b].astype(F32) * quality
                 if n < nch:
-                    first = total - value
-                    first_ref[rows_of(n), block(b)] = first
-                    sums(n + nch, b, (first * quality).astype(BF16))
+                    total1_ref[rows_of(n), block(b)] = full[n][b]
+                    sums(n + nch, b, ((total - value) * quality).astype(BF16))
                 else:
-                    second_ref[rows_of(n), block(b)] = 2.0 * (total - first_ref[rows_of(n), block(b)]) - value
+                    total2_ref[rows_of(n), block(b)] = full[n][b]
             return carry
 
         lax.fori_loop(0, blk // 8, body, 0)
 
-    def begin(n):
-        z_start(n, 1, 0)
-        z_start(n, 1, 1)
-        y_stage(n, 0)
-
+    for load in loads:
+        load.wait()
     first_sums(0)
+    pl.semaphore_wait(barrier, len(partners))
     z_start(0, 1, 0)
     z_start(0, 1, 1)
+    for r in range(1, ny):
+        ask_copy(r).start()
     for n in range(1, nch):
         first_sums(n)
     for r in range(1, ny):
@@ -229,8 +230,8 @@
     y_stage(0, 0)
 
     events = [(d, k) for d in range(1, deep) for k in (0, 1)]
+    last = len(events) - 1
     for n in range(nset):
-        posts = {0: post_a, min(2, len(events) - 1): post_b}
         for e, (d, k) in enumerate(events):
             z_wait(n, d, k)
             z_start(n, d + 1, k)
@@ -238,13 +239,15 @@
                 y_stage(n, d)
             if n > 0:
                 if e == 0:
+                    y_stage(n, 0)
                     post_a(n - 1)
-                if e == min(2, len(events) - 1):
+                if e == min(2, last):
                     post_b(n - 1)
-                if e == min(4, len(events) - 1):
+                if e == min(4, last):
                     post_c(n - 1)
-        if n + 1 < nset:
-            begin(n + 1)
+            if e == min(4, last) and n + 1 < nset:
+                z_start(n + 1, 1, 0)
+                z_start(n + 1, 1, 1)
         z_wait(n, deep, 0)
         y_stage(n, deep)
     post_a(nset - 1)
@@ -294,11 +297,12 @@
     def blocks(count):
         return [pltpu.VMEM((count, CH, 128), BF16)] * nset
 
+    hbm = pl.BlockSpec(memory_space=pltpu.HBM)
     vmem = pl.BlockSpec(memory_space=pltpu.VMEM)
-    return pl.pallas_call(
+    total1, total2 = pl.pallas_call(
         functools.partial(kernel, nz, ny, ncol, blk, knn, nch),
-        out_shape=[jax.ShapeDtypeStruct(probes.shape, F32)] * 2,
-        in_specs=[pl.BlockSpec(memory_space=pltpu.SMEM), vmem, vmem, vmem, vmem],
+        out_shape=[jax.ShapeDtypeStruct(probes.shape, BF16)] * 2,
+        in_specs=[pl.BlockSpec(memory_space=pltpu.SMEM), vmem, hbm, hbm, hbm],
         out_specs=[vmem, vmem],
         scratch_shapes=blocks(blk) * nz
         + blocks((ny - 1) * nz * 8)
@@ -308,6 +312,10 @@
         + blocks(piece)
         + blocks(blk)
         + [
+            pltpu.VMEM(embeddings.shape, BF16),
+            pltpu.VMEM((blk, 128), F32),
+            pltpu.VMEM(probes.shape, F32),
+            pltpu.SemaphoreType.DMA((3,)),
             pltpu.VMEM((ny, 8, 128), jnp.int32),
             pltpu.SMEM((ny, 8, 128), jnp.int32),
             pltpu.SemaphoreType.DMA((nset, 2 * nz)),
@@ -321,14 +329,17 @@
             pltpu.SemaphoreType.DMA,
         ],
         compiler_params=pltpu.CompilerParams(
-            collective_id=0, has_side_effects=True, vmem_limit_bytes=56 * 1024 * 1024),
+            collective_id=0, has_side_effects=True, vmem_limit_bytes=58 * 1024 * 1024),
     )(index, request, embeddings, quality.reshape(blk, 128), probes)
+    first = total1.astype(F32) * quality[None, :] - probes
+    second = 2.0 * (total2.astype(F32) * quality[None, :] - first) - probes
+    return first, second
 
 
 def solution(mesh):
     placed = (P("row", "col"), P("row"), P(None, "row"), P("row", None))
     return jax.shard_map(
-        lambda *arrays: tuple(body(*arrays)),
+        body,
         mesh=mesh,
         in_specs=placed,
         out_specs=(P(None, "row"), P(None, "row")),

time: 121 us -> 118 us (0.975)
  local copies, waits for them, and re-layouts: 4.89 us -> 1.66 us
  Pallas kernels: 114 us -> 111 us
  other arithmetic: 1.02 us -> 3.81 us
    unnamed x5, local copies, waits for them, and re-layouts: 4.1 us -> 0.86 us
    pallas_call x1, Pallas kernels: 114 us -> 111 us  [body(): pl.pallas_call(functools.partial(kernel, nz, ny, ncol, blk, knn, nch), ou...]
    sub x0 -> x1, other arithmetic: none -> 2.79 us  [body(): second = 2.0 * (total2.astype(F32) * quality[None, :] - first) - probes]
where the time goes in v2:
time: 118 us
  Pallas kernels  111 us (94%)
  other arithmetic  3.81 us (3%)
  local copies, waits for them, and re-layouts  1.66 us (1%)
    pallas_call x1, Pallas kernels, body(): pl.pallas_call(functools.partial(kernel, nz, ny, ncol, blk, knn, nch), ou...  111 us
    sub x1, other arithmetic, body(): second = 2.0 * (total2.astype(F32) * quality[None, :] - first) - probes  2.79 us

profile of v2, /device:TPU:1, one launch (start us, length us, event | category | flops | bytes accessed | tf_op | source)
XLA Modules:
  0.0 117.5 jit_solution(5973263024158763508)
XLA Ops:
  0.6 0.0 copy-start
  0.6 0.0 copy-start.1
  0.7 0.9 copy.7
  1.5 0.1 reshape.168
  1.6 0.2 convert_reduce_fusion
  1.8 0.6 add_select_fusion.6
  2.4 0.2 select_reduce_fusion
  2.6 0.1 reshape.169
  2.7 0.6 pad.4.req_ref
  3.3 111.4 %shard_map.59 = (bf16[32,8192]{1,0:T(8,128)(2,1)}, bf16[32,8192]{1,0:T(8,128)(2,1)}) custom-call(s32[512]{0:T(512)} %get-tuple-element.8.idx_ref, s32[4,8,128]{2,1,0:T(8,128)} %pad.4.req_ref, bf16[8192,128]{1,0:T(8,128)(2,1)} %emb_hbm.1, f32[64,128]{1,0:T(8,128)} %bitcast.1, f32[32,8192]{1,0:T(8,128)} %v_hbm.1), custom_call_target="tpu_custom_call" | custom-call | tf_op jit(solution)/shard_map/pallas_call | solution.py:302
  114.7 0.0 copy-done
  114.7 0.0 copy-done.1
  114.7 2.8 %multiply_subtract_fusion = (f32[32,8192]{1,0:T(8,128)}, f32[32,8192]{1,0:T(8,128)}) fusion(f32[32,8192]{1,0:T(8,128)S(1)} %copy-done, bf16[32,8192]{1,0:T(8,128)(2,1)} %get-tuple-element.5, f32[8192]{0:T(1024)S(1)} %copy-done.1, bf16[32,8192]{1,0:T(8,128)(2,1)} %get-tuple-element.4), kind=kLoop, calls=%fused_computation | loop fusion | flops 2097152 | bytes 4227072 | tf_op jit(solution)/shard_map/sub | solution.py:335
  (1 shorter events, 0.0 us)
Async XLA Ops:
  0.6 114.1 %copy-start = (f32[32,8192]{1,0:T(8,128)S(1)}, f32[32,8192]{1,0:T(8,128)}, u32[]{:S(2)}) copy-start(f32[32,8192]{1,0:T(8,128)} %v_hbm.1) | copy-start | bytes 3145732
  0.6 114.1 %copy-start.1 = (f32[8192]{0:T(1024)S(1)}, f32[8192]{0:T(1024)}, u32[]{:S(2)}) copy-start(f32[8192]{0:T(1024)} %param.5) | copy-start | bytes 98308

commit v3 on v2

v3 whole, which is shorter than its diff:
```python
import functools

import jax
import jax.numpy as jnp
from jax import lax
from jax.experimental import pallas as pl
from jax.experimental.pallas import tpu as pltpu
from jax.sharding import PartitionSpec as P

MESH = pl.DeviceIdType.MESH
NY = 4
CH = 16
F32 = jnp.float32
BF16 = jnp.bfloat16


def kernel(nz, ny, ncol, blk, knn, nch, near_hbm, emb_hbm, q_hbm, v_hbm, total1_ref, total2_ref, *scratch):
    scratch = list(scratch)
    nset = 2 * nch
    deep = nz // 2
    half = blk // 2
    piece = blk // ncol
    quart = piece // 2
    slots = [[scratch.pop(0) for _ in range(nz)] for _ in range(nset)]
    stage = [scratch.pop(0) for _ in range(nset)]
    table = [scratch.pop(0) for _ in range(nset)]
    part = [scratch.pop(0) for _ in range(nset)]
    recv = [scratch.pop(0) for _ in range(nset)]
    mine = [scratch.pop(0) for _ in range(nset)]
    full = [scratch.pop(0) for _ in range(nset)]
    near_ref, turned, emb_ref, q_ref, v_ref, load_sem, wide, idx_vmem, idx, ask_vmem, ask, z_send, z_recv, y_send, y_recv, x_send, x_recv, ask_send, ask_recv, ask_sem = scratch

    step = emb_ref.shape[0] // 4
    pairs = [(q_hbm, q_ref), (v_hbm.at[0:CH], v_ref.at[0:CH])]
    pairs += [(emb_hbm.at[pl.ds(i * step, step)], emb_ref.at[pl.ds(i * step, step)]) for i in range(4)]
    pairs += [(v_hbm.at[CH:], v_ref.at[CH:]), (near_hbm, near_ref)]
    loads = [pltpu.make_async_copy(src, dst, load_sem.at[i]) for i, (src, dst) in enumerate(pairs)]
    for load in loads:
        load.start()

    row, col = lax.axis_index("row"), lax.axis_index("col")
    z, y = row // ny, row % ny
    up = (lax.rem(z + 1, nz) * ny + y, col)
    down = (lax.rem(z + nz - 1, nz) * ny + y, col)

    def mate(m):
        return (z * ny + lax.rem(y + m, ny), col)

    x, core = col // 2, col % 2
    others = [(dx, dc) for dx in (2, 1, 3) for dc in (0, 1)] + [(0, 1)]

    def peer(dx, dc):
        return lax.rem(x + dx, 4) * 2 + lax.rem(core + dc, 2)

    def place(dx, dc):
        return lax.rem(4 - dx, 4) * 2 + dc - 1

    barrier = pltpu.get_barrier_semaphore()
    partners = [up, down] + [mate(m) for m in range(1, ny)] + [(row, peer(*o)) for o in others]
    for device in partners:
        pl.semaphore_signal(barrier, inc=1, device_id=device, device_id_type=MESH)

    def make_tables():
        i32 = jnp.int32
        wide[...] = jnp.full(wide.shape, -1, i32)
        wide[:, 0:blk] = near_ref[...]
        ids = wide[...]
        owner, local = ids >> (blk.bit_length() - 1), ids & (blk - 1)
        delta = ((owner >> (ny.bit_length() - 1)) - z + nz) & (nz - 1)
        r = ((owner & (ny - 1)) - y + ny) & (ny - 1)
        p = jnp.where(delta < deep, 2 * delta, 2 * (nz - delta) - 1)
        own = owner == row
        start = jnp.where(own, ny * nz * 8 + local, (r * nz + p) * 8)
        shape = (nz * ny, 128)
        sub, lane = lax.broadcasted_iota(i32, shape, 0), lax.broadcasted_iota(i32, shape, 1)
        seen = jnp.zeros(shape, i32)
        picks = [jnp.zeros(shape, i32) for _ in range(8)]
        for k in range(knn):
            hit = jnp.where(sub == jnp.broadcast_to(owner[k:k + 1], shape), 1, 0)
            upto = hit
            shift = 1
            while shift < blk:
                upto = upto + jnp.where(lane >= shift, pltpu.roll(upto, shift, 1), 0)
                shift *= 2
            rank = jnp.sum(hit * (upto - hit + seen), axis=0, keepdims=True)
            seen = seen + jnp.broadcast_to(upto[:, blk - 1:blk], shape)
            idx_vmem[k:k + 1, :] = start[k:k + 1] + jnp.where(own[k:k + 1], 0, jnp.minimum(rank, 7))
            named = hit * jnp.broadcast_to(local[k:k + 1], shape)
            for t in range(8):
                picks[t] = picks[t] + jnp.where(jnp.broadcast_to(rank, shape) == t, named, 0)
        asked = jnp.zeros(shape, i32)
        for t in range(8):
            asked = jnp.where(lane == t, jnp.sum(picks[t], axis=1, keepdims=True), asked)
        asked = jnp.concatenate([asked, jnp.zeros((128 - nz * ny, 128), i32)], axis=0)
        ask_vmem[0] = jnp.transpose(asked)[0:8]

    def ask_copy(r):
        return pltpu.make_async_remote_copy(
            src_ref=ask_vmem.at[0], dst_ref=ask_vmem.at[ny - r],
            send_sem=ask_send.at[r], recv_sem=ask_recv.at[ny - r],
            device_id=mate(r), device_id_type=MESH)

    def block(b):
        return pl.ds(pl.multiple_of(b * 128, 128), 128)

    def rows_of(n):
        return pl.ds((n % nch) * CH, CH)

    def sums(n, b, weights):
        value = jnp.dot(weights, emb_ref[block(b), :], preferred_element_type=F32).astype(BF16)
        slots[n][0][b] = value
        table[n][ny * nz * 8 + b] = value

    def first_sums(n):
        def body(g, carry):
            for i in range(8):
                b = g * 8 + i
                scaled = (v_ref[rows_of(n), block(b)] * q_ref[pl.ds(b, 1), :]).astype(BF16)
                sums(n, b, scaled)
            return carry

        for i in range(4):
            if n == 0:
                loads[2 + i].wait()
            lax.fori_loop(i * blk // 32, (i + 1) * blk // 32, body, 0)

    def slot_of(d, upward):
        if d == 0:
            return 0
        return nz - 1 if d == deep else (2 * d - 1 if upward else 2 * d)

    def z_copy(n, d, k, upward):
        h = k if upward else 1 - k
        part_of = pl.ds(h * half, half)
        sem = ((d - 1) * 2 + k) * 2 + int(upward)
        return pltpu.make_async_remote_copy(
            src_ref=slots[n][slot_of(d - 1, upward)].at[part_of],
            dst_ref=slots[n][slot_of(d, upward)].at[part_of],
            send_sem=z_send.at[n, sem], recv_sem=z_recv.at[n, sem],
            device_id=up if upward else down, device_id_type=MESH)

    def z_start(n, d, k):
        if d < deep or (d == deep and k == 0):
            for upward in (True, False):
                z_copy(n, d, k, upward).start()

    def z_wait(n, d, k):
        for upward in (True, False):
            z_copy(n, d, k, upward).wait_recv()

    def group(d):
        if d == 0:
            return (0,)
        return (nz - 1,) if d == deep else (2 * d - 1, 2 * d)

    def owner_of(p):
        step = nz - (p + 1) // 2 if p % 2 else p // 2
        return lax.rem(z + step, nz) * ny + y

    def y_stage(n, d):
        ps = group(d)

        def body(t, carry):
            for p in ps:
                for m in range(ny):
                    value = slots[n][p][ask[m, t, owner_of(p)]]
                    if m == 0:
                        table[n][p * 8 + t] = value
                    else:
                        stage[n][((m - 1) * nz + p) * 8 + t] = value
            return carry

        lax.fori_loop(0, 8, body, 0)
        rows = len(ps) * 8
        for m in range(1, ny):
            pltpu.make_async_remote_copy(
                src_ref=stage[n].at[pl.ds(((m - 1) * nz + ps[0]) * 8, rows)],
                dst_ref=table[n].at[pl.ds(((ny - m) * nz + ps[0]) * 8, rows)],
                send_sem=y_send.at[n], recv_sem=y_recv.at[n],
                device_id=mate(m), device_id_type=MESH).start()

    def y_all(n):
        return pltpu.make_async_remote_copy(
            src_ref=stage[n], dst_ref=table[n].at[pl.ds(nz * 8, (ny - 1) * nz * 8)],
            send_sem=y_send.at[n], recv_sem=y_recv.at[n],
            device_id=mate(1), device_id_type=MESH)

    def turn(first_block, count):
        def body(g, carry):
            for i in range(4):
                b = first_block + g * 4 + i
                turned[block(b), :] = jnp.transpose(emb_ref[block(b), :])
            return carry

        lax.fori_loop(0, count // 4, body, 0)

    def partial_rows(n, first_block):
        for i in range(quart):
            b = first_block + i
            total = table[n][idx[0, b]].astype(F32)
            for k in range(1, knn):
                total += table[n][idx[k, b]].astype(F32)
            part[n][b] = jnp.dot(total.astype(BF16), turned[block(b), :], preferred_element_type=F32).astype(BF16)

    def scatter_copy(n, h, dx, dc):
        return pltpu.make_async_remote_copy(
            src_ref=part[n].at[pl.ds(peer(dx, dc) * piece + h * quart, quart)],
            dst_ref=recv[n].at[pl.ds(place(dx, dc) * piece + h * quart, quart)],
            send_sem=x_send.at[n, h], recv_sem=x_recv.at[n, h],
            device_id=(row, peer(dx, dc)), device_id_type=MESH)

    def gather_copy(n, h, dx, dc):
        return pltpu.make_async_remote_copy(
            src_ref=mine[n].at[pl.ds(h * quart, quart)],
            dst_ref=full[n].at[pl.ds(col * piece + h * quart, quart)],
            send_sem=x_send.at[n, 2 + h], recv_sem=x_recv.at[n, 2 + h],
            device_id=(row, peer(dx, dc)), device_id_type=MESH)

    def x_all(n, sem):
        rows = pl.ds(0, (ncol - 1) * quart)
        return pltpu.make_async_remote_copy(
            src_ref=part[n].at[rows], dst_ref=(recv[n] if sem < 2 else full[n]).at[rows],
            send_sem=x_send.at[n, sem], recv_sem=x_recv.at[n, sem],
            device_id=(row, peer(0, 1)), device_id_type=MESH)

    def post_a(n, h):
        if h == 0:
            y_all(n).wait_recv()

        def body(i, carry):
            dx = jnp.where(i == 0, 2, jnp.where(i == 1, 1, 3))
            for dc in (0, 1):
                partial_rows(n, peer(dx, dc) * piece + h * quart)
            for dc in (0, 1):
                scatter_copy(n, h, dx, dc).start()
            return carry

        lax.fori_loop(0, 3, body, 0)
        partial_rows(n, peer(0, 1) * piece + h * quart)
        partial_rows(n, col * piece + h * quart)
        scatter_copy(n, h, 0, 1).start()

    def post_b(n, h):
        x_all(n, h).wait_recv()
        for i in range(h * quart, (h + 1) * quart):
            total = part[n][col * piece + i].astype(F32)
            for r in range(1, ncol):
                total += recv[n][(r - 1) * piece + i].astype(F32)
            total = total.astype(BF16)
            mine[n][i] = total
            full[n][col * piece + i] = total
        for dx, dc in others:
            gather_copy(n, h, dx, dc).start()

    def post_c(n):
        for h in (0, 1):
            x_all(n, 2 + h).wait_recv()

        def body(g, carry):
            for i in range(8):
                b = g * 8 + i
                quality = q_ref[pl.ds(b, 1), :]
                value = v_ref[rows_of(n), block(b)]
                total = full[n][b].astype(F32) * quality
                if n < nch:
                    total1_ref[rows_of(n), block(b)] = full[n][b]
                    sums(n + nch, b, ((total - value) * quality).astype(BF16))
                else:
                    total2_ref[rows_of(n), block(b)] = full[n][b]
            return carry

        lax.fori_loop(0, blk // 8, body, 0)

    for load in loads[:2]:
        load.wait()
    first_sums(0)
    for load in loads[6:]:
        load.wait()
    pl.semaphore_wait(barrier, len(partners))
    z_start(0, 1, 0)
    z_start(0, 1, 1)
    make_tables()
    for r in range(1, ny):
        ask_copy(r).start()
    for n in range(1, nch):
        first_sums(n)
    to_smem = [pltpu.make_async_copy(idx_vmem, idx, ask_sem.at[0]), pltpu.make_async_copy(ask_vmem, ask, ask_sem.at[1])]

    events = [(d, k) for d in range(1, deep) for k in (0, 1)]
    for n in range(nset):
        for e, (d, k) in enumerate(events):
            z_wait(n, d, k)
            z_start(n, d + 1, k)
            if n == 0 and e == 0:
                for r in range(1, ny):
                    ask_copy(r).wait_recv()
                for copy in to_smem:
                    copy.start()
            if n == 0 and e == 1:
                for copy in to_smem:
                    copy.wait()
                y_stage(0, 0)
            if k == 1:
                y_stage(n, d)
            if n == 0 and e < 4:
                turn(e * blk // 4, blk // 4)
            if n > 0:
                if e == 0:
                    y_stage(n, 0)
                    post_a(n - 1, 0)
                if e == 1:
                    post_a(n - 1, 1)
                    post_b(n - 1, 0)
                if e == 2:
                    post_b(n - 1, 1)
                if e == 4:
                    post_c(n - 1)
            if e == 4 and n + 1 < nset:
                z_start(n + 1, 1, 0)
                z_start(n + 1, 1, 1)
        z_wait(n, deep, 0)
        y_stage(n, deep)
    post_a(nset - 1, 0)
    post_a(nset - 1, 1)
    post_b(nset - 1, 0)
    post_b(nset - 1, 1)
    post_c(nset - 1)

    for r in range(1, ny):
        ask_copy(r).wait_send()
    for n in range(nset):
        for d in range(1, deep + 1):
            for k in (0, 1):
                if d < deep or k == 0:
                    for upward in (True, False):
                        z_copy(n, d, k, upward).wait_send()
        y_all(n).wait_send()
        for sem in range(4):
            x_all(n, sem).wait_send()


def body(embeddings, quality, probes, neighbors, ny=NY, ncol=8, nz=8):
    blk, knn = neighbors.shape
    nch = probes.shape[0] // CH
    nset = 2 * nch
    piece = blk // ncol

    def blocks(count):
        return [pltpu.VMEM((count, CH, 128), BF16)] * nset

    hbm = pl.BlockSpec(memory_space=pltpu.HBM)
    vmem = pl.BlockSpec(memory_space=pltpu.VMEM)
    total1, total2 = pl.pallas_call(
        functools.partial(kernel, nz, ny, ncol, blk, knn, nch),
        out_shape=[jax.ShapeDtypeStruct(probes.shape, BF16)] * 2,
        in_specs=[hbm] * 4,
        out_specs=[vmem, vmem],
        scratch_shapes=blocks(blk) * nz
        + blocks((ny - 1) * nz * 8)
        + blocks(ny * nz * 8 + blk)
        + blocks(blk)
        + blocks((ncol - 1) * piece)
        + blocks(piece)
        + blocks(blk)
        + [
            pltpu.VMEM((knn, blk), jnp.int32),
            pltpu.VMEM(embeddings.shape, BF16),
            pltpu.VMEM(embeddings.shape, BF16),
            pltpu.VMEM((blk, 128), F32),
            pltpu.VMEM(probes.shape, F32),
            pltpu.SemaphoreType.DMA((8,)),
            pltpu.VMEM((knn, 128), jnp.int32),
            pltpu.VMEM((knn, 128), jnp.int32),
            pltpu.SMEM((knn, 128), jnp.int32),
            pltpu.VMEM((ny, 8, 128), jnp.int32),
            pltpu.SMEM((ny, 8, 128), jnp.int32),
            pltpu.SemaphoreType.DMA((nset, 2 * nz)),
            pltpu.SemaphoreType.DMA((nset, 2 * nz)),
            pltpu.SemaphoreType.DMA((nset,)),
            pltpu.SemaphoreType.DMA((nset,)),
            pltpu.SemaphoreType.DMA((nset, 4)),
            pltpu.SemaphoreType.DMA((nset, 4)),
            pltpu.SemaphoreType.DMA((ny,)),
            pltpu.SemaphoreType.DMA((ny,)),
            pltpu.SemaphoreType.DMA((2,)),
        ],
        compiler_params=pltpu.CompilerParams(
            collective_id=0, has_side_effects=True, vmem_limit_bytes=36 * 1024 * 1024),
    )(*[pltpu.with_memory_space_constraint(array, pltpu.HBM)
        for array in (neighbors.T, embeddings, quality.reshape(blk, 128), probes)])
    first = total1.astype(F32) * quality[None, :] - probes
    second = 2.0 * (total2.astype(F32) * quality[None, :] - first) - probes
    return first, second


def solution(mesh):
    placed = (P("row", "col"), P("row"), P(None, "row"), P("row", None))
    return jax.shard_map(
        body,
        mesh=mesh,
        in_specs=placed,
        out_specs=(P(None, "row"), P(None, "row")),
        check_vma=False,
    )
```

time: 118 us -> 112 us (0.949)
  other arithmetic: 3.81 us -> 1.59 us
  local copies, waits for them, and re-layouts: 1.66 us -> 0.01 us
    pallas_call x1, Pallas kernels: 111 us -> 110 us  [body(): pl.pallas_call(functools.partial(kernel, nz, ny, ncol, blk, knn, nch), ou...]
    sub x1, other arithmetic: 2.79 us -> 1.59 us  [body(): second = 2.0 * (total2.astype(F32) * quality[None, :] - first) - probes]
where the time goes in v3:
time: 112 us
  Pallas kernels  110 us (98%)
  other arithmetic  1.59 us (1%)
    pallas_call x1, Pallas kernels, body(): pl.pallas_call(functools.partial(kernel, nz, ny, ncol, blk, knn, nch), ou...  110 us

profile of v3, /device:TPU:1, one launch (start us, length us, event | category | flops | bytes accessed | tf_op | source)
XLA Modules:
  0.0 111.8 jit_solution(15229022999563877274)
XLA Ops:
  0.6 0.0 copy-start
  0.6 0.0 copy-start.1
  0.7 109.6 %shard_map.59 = (bf16[32,8192]{1,0:T(8,128)(2,1)S(1)}, bf16[32,8192]{1,0:T(8,128)(2,1)S(1)}) custom-call(s32[8,64]{1,0:T(8,128)} %bitcast.3, bf16[8192,128]{1,0:T(8,128)(2,1)} %emb_hbm.1, f32[64,128]{1,0:T(8,128)} %bitcast.2, f32[32,8192]{1,0:T(8,128)} %v_hbm.1), custom_call_target="tpu_custom_call" | custom-call | tf_op jit(solution)/shard_map/pallas_call | solution.py:353
  110.2 0.0 copy-done
  110.2 0.0 copy-done.1
  110.2 1.6 %multiply_subtract_fusion = (f32[32,8192]{1,0:T(8,128)}, f32[32,8192]{1,0:T(8,128)}) fusion(f32[32,8192]{1,0:T(8,128)S(1)} %copy-done, bf16[32,8192]{1,0:T(8,128)(2,1)S(1)} %get-tuple-element.5, f32[8192]{0:T(1024)S(1)} %copy-done.1, bf16[32,8192]{1,0:T(8,128)(2,1)S(1)} %get-tuple-element.4), kind=kLoop, calls=%fused_computation | loop fusion | flops 2097152 | bytes 4227072 | tf_op jit(solution)/shard_map/sub | solution.py:392
Async XLA Ops:
  0.6 109.6 %copy-start = (f32[32,8192]{1,0:T(8,128)S(1)}, f32[32,8192]{1,0:T(8,128)}, u32[]{:S(2)}) copy-start(f32[32,8192]{1,0:T(8,128)} %v_hbm.1) | copy-start | bytes 3145732
  0.6 109.6 %copy-start.1 = (f32[8192]{0:T(1024)S(1)}, f32[8192]{0:T(1024)}, u32[]{:S(2)}) copy-start(f32[8192]{0:T(1024)} %param.5) | copy-start | bytes 98308

commit v4 on v3

--- a/solution.py
+++ b/solution.py
@@ -14,7 +14,7 @@
 BF16 = jnp.bfloat16
 
 
-def kernel(nz, ny, ncol, blk, knn, nch, near_hbm, emb_hbm, q_hbm, v_hbm, total1_ref, total2_ref, *scratch):
+def kernel(nz, ny, ncol, blk, knn, nch, near_hbm, emb_hbm, q_hbm, v_hbm, total1_out, total2_out, *scratch):
     scratch = list(scratch)
     nset = 2 * nch
     deep = nz // 2
@@ -28,11 +28,14 @@
     recv = [scratch.pop(0) for _ in range(nset)]
     mine = [scratch.pop(0) for _ in range(nset)]
     full = [scratch.pop(0) for _ in range(nset)]
-    near_ref, turned, emb_ref, q_ref, v_ref, load_sem, wide, idx_vmem, idx, ask_vmem, ask, z_send, z_recv, y_send, y_recv, x_send, x_recv, ask_send, ask_recv, ask_sem = scratch
+    total1_ref, total2_ref, out_sem, near_ref, turned, emb_ref, q_ref, v_ref, load_sem, wide, idx_vmem, idx, ask_vmem, ask, z_send, z_recv, y_send, y_recv, x_send, x_recv, ask_send, ask_recv, ask_sem = scratch
 
     step = emb_ref.shape[0] // 4
-    pairs = [(q_hbm, q_ref), (v_hbm.at[0:CH], v_ref.at[0:CH])]
-    pairs += [(emb_hbm.at[pl.ds(i * step, step)], emb_ref.at[pl.ds(i * step, step)]) for i in range(4)]
+    quarters = (0, 2, 1, 3)
+    pairs = [(q_hbm, q_ref)]
+    for i in quarters:
+        docs = pl.ds(i * step, step)
+        pairs += [(v_hbm.at[0:CH, docs], v_ref.at[0:CH, docs]), (emb_hbm.at[docs], emb_ref.at[docs])]
     pairs += [(v_hbm.at[CH:], v_ref.at[CH:]), (near_hbm, near_ref)]
     loads = [pltpu.make_async_copy(src, dst, load_sem.at[i]) for i, (src, dst) in enumerate(pairs)]
     for load in loads:
@@ -111,42 +114,46 @@
         slots[n][0][b] = value
         table[n][ny * nz * 8 + b] = value
 
-    def first_sums(n):
+    def first_sums(n, i):
         def body(g, carry):
-            for i in range(8):
-                b = g * 8 + i
+            for j in range(8):
+                b = g * 8 + j
                 scaled = (v_ref[rows_of(n), block(b)] * q_ref[pl.ds(b, 1), :]).astype(BF16)
                 sums(n, b, scaled)
             return carry
 
-        for i in range(4):
-            if n == 0:
-                loads[2 + i].wait()
-            lax.fori_loop(i * blk // 32, (i + 1) * blk // 32, body, 0)
+        lax.fori_loop(i * blk // 32, (i + 1) * blk // 32, body, 0)
 
     def slot_of(d, upward):
         if d == 0:
             return 0
         return nz - 1 if d == deep else (2 * d - 1 if upward else 2 * d)
 
-    def z_copy(n, d, k, upward):
-        h = k if upward else 1 - k
-        part_of = pl.ds(h * half, half)
-        sem = ((d - 1) * 2 + k) * 2 + int(upward)
-        return pltpu.make_async_remote_copy(
-            src_ref=slots[n][slot_of(d - 1, upward)].at[part_of],
-            dst_ref=slots[n][slot_of(d, upward)].at[part_of],
+    def z_copy(n, d, k, upward, first, count, sem):
+        rows = pl.ds((k if upward else 1 - k) * half + first, count)
+        return pltpu.make_async_remote_copy(
+            src_ref=slots[n][slot_of(d - 1, upward)].at[rows],
+            dst_ref=slots[n][slot_of(d, upward)].at[rows],
             send_sem=z_send.at[n, sem], recv_sem=z_recv.at[n, sem],
             device_id=up if upward else down, device_id_type=MESH)
+
+    def z_parts(n, d, k, upward):
+        sem = ((d - 1) * 2 + k) * 2 + int(upward)
+        if (n, d, k) == (0, 1, 0):
+            return [z_copy(n, d, k, upward, 0, half // 2, sem),
+                    z_copy(n, d, k, upward, half // 2, half // 2, 14 + int(upward))]
+        return [z_copy(n, d, k, upward, 0, half, sem)]
 
     def z_start(n, d, k):
         if d < deep or (d == deep and k == 0):
             for upward in (True, False):
-                z_copy(n, d, k, upward).start()
+                for copy in z_parts(n, d, k, upward):
+                    copy.start()
 
     def z_wait(n, d, k):
         for upward in (True, False):
-            z_copy(n, d, k, upward).wait_recv()
+            for copy in z_parts(n, d, k, upward):
+                copy.wait_recv()
 
     def group(d):
         if d == 0:
@@ -172,7 +179,7 @@
 
         lax.fori_loop(0, 8, body, 0)
         rows = len(ps) * 8
-        for m in range(1, ny):
+        for m in (2, 1, 3):
             pltpu.make_async_remote_copy(
                 src_ref=stage[n].at[pl.ds(((m - 1) * nz + ps[0]) * 8, rows)],
                 dst_ref=table[n].at[pl.ds(((ny - m) * nz + ps[0]) * 8, rows)],
@@ -251,6 +258,10 @@
             full[n][col * piece + i] = total
         for dx, dc in others:
             gather_copy(n, h, dx, dc).start()
+
+    def out_copy(n):
+        source, target = (total1_ref, total1_out) if n < nch else (total2_ref, total2_out)
+        return pltpu.make_async_copy(source.at[rows_of(n)], target.at[rows_of(n)], out_sem.at[n])
 
     def post_c(n):
         for h in (0, 1):
@@ -270,21 +281,38 @@
             return carry
 
         lax.fori_loop(0, blk // 8, body, 0)
-
-    for load in loads[:2]:
+        out_copy(n).start()
+
+    loads[0].wait()
+    for turn_of, i in enumerate(quarters):
+        loads[1 + 2 * turn_of].wait()
+        loads[2 + 2 * turn_of].wait()
+        first_sums(0, i)
+        if turn_of == 0:
+            pl.semaphore_wait(barrier, len(partners))
+        z_parts(0, 1, 0, i < 2)[i % 2].start()
+    z_start(0, 1, 1)
+    for load in loads[9:]:
         load.wait()
-    first_sums(0)
-    for load in loads[6:]:
-        load.wait()
-    pl.semaphore_wait(barrier, len(partners))
-    z_start(0, 1, 0)
-    z_start(0, 1, 1)
     make_tables()
     for r in range(1, ny):
         ask_copy(r).start()
     for n in range(1, nch):
-        first_sums(n)
+        for i in range(4):
+            first_sums(n, i)
     to_smem = [pltpu.make_async_copy(idx_vmem, idx, ask_sem.at[0]), pltpu.make_async_copy(ask_vmem, ask, ask_sem.at[1])]
+
+    def sent(n):
+        for d in range(1, deep + 1):
+            for k in (0, 1):
+                if d < deep or k == 0:
+                    for upward in (True, False):
+                        for copy in z_parts(n, d, k, upward):
+                            copy.wait_send()
+        y_all(n).wait_send()
+        for sem in range(4):
+            x_all(n, sem).wait_send()
+        out_copy(n).wait()
 
     events = [(d, k) for d in range(1, deep) for k in (0, 1)]
     for n in range(nset):
@@ -307,19 +335,21 @@
             if n > 0:
                 if e == 0:
                     y_stage(n, 0)
+                if e == 1:
                     post_a(n - 1, 0)
-                if e == 1:
                     post_a(n - 1, 1)
+                if e == (3 if n == nset - 1 else 2):
                     post_b(n - 1, 0)
-                if e == 2:
                     post_b(n - 1, 1)
-                if e == 4:
+                if e == (5 if n == nset - 1 else 4):
                     post_c(n - 1)
             if e == 4 and n + 1 < nset:
                 z_start(n + 1, 1, 0)
                 z_start(n + 1, 1, 1)
         z_wait(n, deep, 0)
         y_stage(n, deep)
+        if n > 0:
+            sent(n - 1)
     post_a(nset - 1, 0)
     post_a(nset - 1, 1)
     post_b(nset - 1, 0)
@@ -328,15 +358,7 @@
 
     for r in range(1, ny):
         ask_copy(r).wait_send()
-    for n in range(nset):
-        for d in range(1, deep + 1):
-            for k in (0, 1):
-                if d < deep or k == 0:
-                    for upward in (True, False):
-                        z_copy(n, d, k, upward).wait_send()
-        y_all(n).wait_send()
-        for sem in range(4):
-            x_all(n, sem).wait_send()
+    sent(nset - 1)
 
 
 def body(embeddings, quality, probes, neighbors, ny=NY, ncol=8, nz=8):
@@ -349,12 +371,11 @@
         return [pltpu.VMEM((count, CH, 128), BF16)] * nset
 
     hbm = pl.BlockSpec(memory_space=pltpu.HBM)
-    vmem = pl.BlockSpec(memory_space=pltpu.VMEM)
     total1, total2 = pl.pallas_call(
         functools.partial(kernel, nz, ny, ncol, blk, knn, nch),
         out_shape=[jax.ShapeDtypeStruct(probes.shape, BF16)] * 2,
         in_specs=[hbm] * 4,
-        out_specs=[vmem, vmem],
+        out_specs=[pl.BlockSpec(memory_space=pl.ANY)] * 2,
         scratch_shapes=blocks(blk) * nz
         + blocks((ny - 1) * nz * 8)
         + blocks(ny * nz * 8 + blk)
@@ -363,12 +384,15 @@
         + blocks(piece)
         + blocks(blk)
         + [
+            pltpu.VMEM(probes.shape, BF16),
+            pltpu.VMEM(probes.shape, BF16),
+            pltpu.SemaphoreType.DMA((nset,)),
             pltpu.VMEM((knn, blk), jnp.int32),
             pltpu.VMEM(embeddings.shape, BF16),
             pltpu.VMEM(embeddings.shape, BF16),
             pltpu.VMEM((blk, 128), F32),
             pltpu.VMEM(probes.shape, F32),
-            pltpu.SemaphoreType.DMA((8,)),
+            pltpu.SemaphoreType.DMA((11,)),
             pltpu.VMEM((knn, 128), jnp.int32),
             pltpu.VMEM((knn, 128), jnp.int32),
             pltpu.SMEM((knn, 128), jnp.int32),

time: 112 us -> 110 us (0.982)
  Pallas kernels: 110 us -> 108 us
    pallas_call x1, Pallas kernels: 110 us -> 108 us  [body(): pl.pallas_call(functools.partial(kernel, nz, ny, ncol, blk, knn, nch), ou...]
where the time goes in v4:
time: 110 us
  Pallas kernels  108 us (98%)
  other arithmetic  1.59 us (1%)
    pallas_call x1, Pallas kernels, body(): pl.pallas_call(functools.partial(kernel, nz, ny, ncol, blk, knn, nch), ou...  108 us

profile of v4, /device:TPU:1, one launch (start us, length us, event | category | flops | bytes accessed | tf_op | source)
XLA Modules:
  0.0 110.2 jit_solution(14319914631059769837)
XLA Ops:
  0.6 0.0 copy-start
  0.6 0.0 copy-start.1
  0.7 108.0 %shard_map.59 = (bf16[32,8192]{1,0:T(8,128)(2,1)S(1)}, bf16[32,8192]{1,0:T(8,128)(2,1)S(1)}) custom-call(s32[8,64]{1,0:T(8,128)} %bitcast.3, bf16[8192,128]{1,0:T(8,128)(2,1)} %emb_hbm.1, f32[64,128]{1,0:T(8,128)} %bitcast.2, f32[32,8192]{1,0:T(8,128)} %v_hbm.1), custom_call_target="tpu_custom_call" | custom-call | tf_op jit(solution)/shard_map/pallas_call | solution.py:374
  108.6 0.0 copy-done
  108.6 0.0 copy-done.1
  108.7 1.6 %multiply_subtract_fusion = (f32[32,8192]{1,0:T(8,128)}, f32[32,8192]{1,0:T(8,128)}) fusion(f32[32,8192]{1,0:T(8,128)S(1)} %copy-done, bf16[32,8192]{1,0:T(8,128)(2,1)S(1)} %get-tuple-element.5, f32[8192]{0:T(1024)S(1)} %copy-done.1, bf16[32,8192]{1,0:T(8,128)(2,1)S(1)} %get-tuple-element.4), kind=kLoop, calls=%fused_computation | loop fusion | flops 2097152 | bytes 4227072 | tf_op jit(solution)/shard_map/sub | solution.py:416
Async XLA Ops:
  0.6 108.0 %copy-start = (f32[32,8192]{1,0:T(8,128)S(1)}, f32[32,8192]{1,0:T(8,128)}, u32[]{:S(2)}) copy-start(f32[32,8192]{1,0:T(8,128)} %v_hbm.1) | copy-start | bytes 3145732
  0.6 108.0 %copy-start.1 = (f32[8192]{0:T(1024)S(1)}, f32[8192]{0:T(1024)}, u32[]{:S(2)}) copy-start(f32[8192]{0:T(1024)} %param.5) | copy-start | bytes 98308

commit v5 on v4

--- a/solution.py
+++ b/solution.py
@@ -28,7 +28,7 @@
     recv = [scratch.pop(0) for _ in range(nset)]
     mine = [scratch.pop(0) for _ in range(nset)]
     full = [scratch.pop(0) for _ in range(nset)]
-    total1_ref, total2_ref, out_sem, near_ref, turned, emb_ref, q_ref, v_ref, load_sem, wide, idx_vmem, idx, ask_vmem, ask, z_send, z_recv, y_send, y_recv, x_send, x_recv, ask_send, ask_recv, ask_sem = scratch
+    total1_ref, total2_ref, out_sem, near_ref, turned, emb_ref, q_ref, v_ref, load_sem, wide, idx_vmem, idx, ask_vmem, ask, z_send, z_recv, y_send, y_recv, x_send, x_recv, p_send, p_recv, ask_send, ask_recv, ask_sem = scratch
 
     step = emb_ref.shape[0] // 4
     quarters = (0, 2, 1, 3)
@@ -134,7 +134,7 @@
         return pltpu.make_async_remote_copy(
             src_ref=slots[n][slot_of(d - 1, upward)].at[rows],
             dst_ref=slots[n][slot_of(d, upward)].at[rows],
-            send_sem=z_send.at[n, sem], recv_sem=z_recv.at[n, sem],
+            send_sem=z_send.at[n, int(upward)], recv_sem=z_recv.at[n % 2, sem],
             device_id=up if upward else down, device_id_type=MESH)
 
     def z_parts(n, d, k, upward):
@@ -213,22 +213,51 @@
         return pltpu.make_async_remote_copy(
             src_ref=part[n].at[pl.ds(peer(dx, dc) * piece + h * quart, quart)],
             dst_ref=recv[n].at[pl.ds(place(dx, dc) * piece + h * quart, quart)],
-            send_sem=x_send.at[n, h], recv_sem=x_recv.at[n, h],
+            send_sem=x_send.at[n % 2, h], recv_sem=x_recv.at[n % 2, h],
             device_id=(row, peer(dx, dc)), device_id_type=MESH)
 
     def gather_copy(n, h, dx, dc):
         return pltpu.make_async_remote_copy(
             src_ref=mine[n].at[pl.ds(h * quart, quart)],
             dst_ref=full[n].at[pl.ds(col * piece + h * quart, quart)],
-            send_sem=x_send.at[n, 2 + h], recv_sem=x_recv.at[n, 2 + h],
+            send_sem=x_send.at[n % 2, 2 + h], recv_sem=x_recv.at[n % 2, 2 + h],
             device_id=(row, peer(dx, dc)), device_id_type=MESH)
 
     def x_all(n, sem):
         rows = pl.ds(0, (ncol - 1) * quart)
         return pltpu.make_async_remote_copy(
             src_ref=part[n].at[rows], dst_ref=(recv[n] if sem < 2 else full[n]).at[rows],
-            send_sem=x_send.at[n, sem], recv_sem=x_recv.at[n, sem],
+            send_sem=x_send.at[n % 2, sem], recv_sem=x_recv.at[n % 2, sem],
             device_id=(row, peer(0, 1)), device_id_type=MESH)
+
+    def ring_copy(n, h, dx):
+        return gather_copy(n, h, dx, 0)
+
+    def ring_all(n, h):
+        rows = pl.ds(0, 3 * quart)
+        return pltpu.make_async_remote_copy(
+            src_ref=part[n].at[rows], dst_ref=full[n].at[rows],
+            send_sem=x_send.at[n % 2, 2 + h], recv_sem=x_recv.at[n % 2, 2 + h],
+            device_id=(row, peer(1, 0)), device_id_type=MESH)
+
+    def pair_copy(n, h, dx):
+        rows = pl.ds(peer(dx, 0) * piece + h * quart, quart)
+        return pltpu.make_async_remote_copy(
+            src_ref=full[n].at[rows] if dx else mine[n].at[pl.ds(h * quart, quart)], dst_ref=full[n].at[rows],
+            send_sem=p_send.at[h], recv_sem=p_recv.at[h],
+            device_id=(row, peer(0, 1)), device_id_type=MESH)
+
+    def pair_all(n, h):
+        rows = pl.ds(0, 4 * quart)
+        return pltpu.make_async_remote_copy(
+            src_ref=part[n].at[rows], dst_ref=full[n].at[rows],
+            send_sem=p_send.at[h], recv_sem=p_recv.at[h],
+            device_id=(row, peer(0, 1)), device_id_type=MESH)
+
+    def hand_on(n, h):
+        ring_all(n, h).wait_recv()
+        for dx in (2, 1, 3):
+            pair_copy(n, h, dx).start()
 
     def post_a(n, h):
         if h == 0:
@@ -256,8 +285,13 @@
             total = total.astype(BF16)
             mine[n][i] = total
             full[n][col * piece + i] = total
-        for dx, dc in others:
-            gather_copy(n, h, dx, dc).start()
+        if n == nset - 1:
+            for dx in (2, 1, 3):
+                ring_copy(n, h, dx).start()
+            pair_copy(n, h, 0).start()
+        else:
+            for dx, dc in others:
+                gather_copy(n, h, dx, dc).start()
 
     def out_copy(n):
         source, target = (total1_ref, total1_out) if n < nch else (total2_ref, total2_out)
@@ -265,7 +299,7 @@
 
     def post_c(n):
         for h in (0, 1):
-            x_all(n, 2 + h).wait_recv()
+            (pair_all(n, h) if n == nset - 1 else x_all(n, 2 + h)).wait_recv()
 
         def body(g, carry):
             for i in range(8):
@@ -303,15 +337,20 @@
     to_smem = [pltpu.make_async_copy(idx_vmem, idx, ask_sem.at[0]), pltpu.make_async_copy(ask_vmem, ask, ask_sem.at[1])]
 
     def sent(n):
-        for d in range(1, deep + 1):
-            for k in (0, 1):
-                if d < deep or k == 0:
-                    for upward in (True, False):
-                        for copy in z_parts(n, d, k, upward):
-                            copy.wait_send()
+        for upward in (True, False):
+            rows = pl.ds(0, (2 * deep - 1) * half)
+            pltpu.make_async_remote_copy(
+                src_ref=table[n].at[rows], dst_ref=table[n].at[rows],
+                send_sem=z_send.at[n, int(upward)], recv_sem=z_recv.at[n % 2, int(upward)],
+                device_id=up if upward else down, device_id_type=MESH).wait_send()
         y_all(n).wait_send()
-        for sem in range(4):
-            x_all(n, sem).wait_send()
+        for h in (0, 1):
+            x_all(n, h).wait_send()
+            if n == nset - 1:
+                ring_all(n, h).wait_send()
+                pair_all(n, h).wait_send()
+            else:
+                x_all(n, 2 + h).wait_send()
         out_copy(n).wait()
 
     events = [(d, k) for d in range(1, deep) for k in (0, 1)]
@@ -354,6 +393,8 @@
     post_a(nset - 1, 1)
     post_b(nset - 1, 0)
     post_b(nset - 1, 1)
+    hand_on(nset - 1, 0)
+    hand_on(nset - 1, 1)
     post_c(nset - 1)
 
     for r in range(1, ny):
@@ -398,12 +439,14 @@
             pltpu.SMEM((knn, 128), jnp.int32),
             pltpu.VMEM((ny, 8, 128), jnp.int32),
             pltpu.SMEM((ny, 8, 128), jnp.int32),
-            pltpu.SemaphoreType.DMA((nset, 2 * nz)),
-            pltpu.SemaphoreType.DMA((nset, 2 * nz)),
+            pltpu.SemaphoreType.DMA((nset, 2)),
+            pltpu.SemaphoreType.DMA((2, 2 * nz)),
             pltpu.SemaphoreType.DMA((nset,)),
             pltpu.SemaphoreType.DMA((nset,)),
-            pltpu.SemaphoreType.DMA((nset, 4)),
-            pltpu.SemaphoreType.DMA((nset, 4)),
+            pltpu.SemaphoreType.DMA((2, 4)),
+            pltpu.SemaphoreType.DMA((2, 4)),
+            pltpu.SemaphoreType.DMA((2,)),
+            pltpu.SemaphoreType.DMA((2,)),
             pltpu.SemaphoreType.DMA((ny,)),
             pltpu.SemaphoreType.DMA((ny,)),
             pltpu.SemaphoreType.DMA((2,)),

time: 110 us -> 109 us (level)
  no operation moved by 1% of the time
where the time goes in v5:
time: 109 us
  Pallas kernels  107 us (98%)
  other arithmetic  1.59 us (1%)
    pallas_call x1, Pallas kernels, body(): pl.pallas_call(functools.partial(kernel, nz, ny, ncol, blk, knn, nch), ou...  107 us

profile of v5, /device:TPU:1, one launch (start us, length us, event | category | flops | bytes accessed | tf_op | source)
XLA Modules:
  0.0 109.3 jit_solution(13925397476587647662)
XLA Ops:
  0.6 0.0 copy-start
  0.6 0.0 copy-start.1
  0.7 107.0 %shard_map.59 = (bf16[32,8192]{1,0:T(8,128)(2,1)S(1)}, bf16[32,8192]{1,0:T(8,128)(2,1)S(1)}) custom-call(s32[8,64]{1,0:T(8,128)} %bitcast.3, bf16[8192,128]{1,0:T(8,128)(2,1)} %emb_hbm.1, f32[64,128]{1,0:T(8,128)} %bitcast.2, f32[32,8192]{1,0:T(8,128)} %v_hbm.1), custom_call_target="tpu_custom_call" | custom-call | tf_op jit(solution)/shard_map/pallas_call | solution.py:415
  107.6 0.0 copy-done
  107.7 0.0 copy-done.1
  107.7 1.6 %multiply_subtract_fusion = (f32[32,8192]{1,0:T(8,128)}, f32[32,8192]{1,0:T(8,128)}) fusion(f32[32,8192]{1,0:T(8,128)S(1)} %copy-done, bf16[32,8192]{1,0:T(8,128)(2,1)S(1)} %get-tuple-element.5, f32[8192]{0:T(1024)S(1)} %copy-done.1, bf16[32,8192]{1,0:T(8,128)(2,1)S(1)} %get-tuple-element.4), kind=kLoop, calls=%fused_computation | loop fusion | flops 2097152 | bytes 4227072 | tf_op jit(solution)/shard_map/sub | solution.py:459
Async XLA Ops:
  0.6 107.0 %copy-start = (f32[32,8192]{1,0:T(8,128)S(1)}, f32[32,8192]{1,0:T(8,128)}, u32[]{:S(2)}) copy-start(f32[32,8192]{1,0:T(8,128)} %v_hbm.1) | copy-start | bytes 3145732
  0.6 107.0 %copy-start.1 = (f32[8192]{0:T(1024)S(1)}, f32[8192]{0:T(1024)}, u32[]{:S(2)}) copy-start(f32[8192]{0:T(1024)} %param.5) | copy-start | bytes 98308

commit v6 on v5

--- a/solution.py
+++ b/solution.py
@@ -314,7 +314,13 @@
                     total2_ref[rows_of(n), block(b)] = full[n][b]
             return carry
 
-        lax.fori_loop(0, blk // 8, body, 0)
+        lax.fori_loop(0, blk // 16, body, 0)
+        if n < nch:
+            z_parts(n + nch, 1, 0, True)[0].start()
+        lax.fori_loop(blk // 16, blk // 8, body, 0)
+        if n < nch:
+            z_parts(n + nch, 1, 0, False)[0].start()
+            z_start(n + nch, 1, 1)
         out_copy(n).start()
 
     loads[0].wait()
@@ -379,10 +385,11 @@
                     post_a(n - 1, 1)
                 if e == (3 if n == nset - 1 else 2):
                     post_b(n - 1, 0)
+                if e == 3:
                     post_b(n - 1, 1)
                 if e == (5 if n == nset - 1 else 4):
                     post_c(n - 1)
-            if e == 4 and n + 1 < nset:
+            if e == 4 and n + 1 < nch:
                 z_start(n + 1, 1, 0)
                 z_start(n + 1, 1, 1)
         z_wait(n, deep, 0)

time: 109 us -> 109 us (level)
  no operation moved by 1% of the time
where the time goes in v6:
time: 109 us
  Pallas kernels  106 us (97%)
  other arithmetic  1.59 us (1%)
    pallas_call x1, Pallas kernels, body(): pl.pallas_call(functools.partial(kernel, nz, ny, ncol, blk, knn, nch), ou...  106 us

profile of v6, /device:TPU:1, one launch (start us, length us, event | category | flops | bytes accessed | tf_op | source)
XLA Modules:
  0.0 108.6 jit_solution(18361417357121275917)
XLA Ops:
  0.6 0.0 copy-start
  0.6 0.0 copy-start.1
  0.7 106.4 %shard_map.59 = (bf16[32,8192]{1,0:T(8,128)(2,1)S(1)}, bf16[32,8192]{1,0:T(8,128)(2,1)S(1)}) custom-call(s32[8,64]{1,0:T(8,128)} %bitcast.3, bf16[8192,128]{1,0:T(8,128)(2,1)} %emb_hbm.1, f32[64,128]{1,0:T(8,128)} %bitcast.2, f32[32,8192]{1,0:T(8,128)} %v_hbm.1), custom_call_target="tpu_custom_call" | custom-call | tf_op jit(solution)/shard_map/pallas_call | solution.py:422
  107.0 0.0 copy-done
  107.0 0.0 copy-done.1
  107.0 1.6 %multiply_subtract_fusion = (f32[32,8192]{1,0:T(8,128)}, f32[32,8192]{1,0:T(8,128)}) fusion(f32[32,8192]{1,0:T(8,128)S(1)} %copy-done, bf16[32,8192]{1,0:T(8,128)(2,1)S(1)} %get-tuple-element.5, f32[8192]{0:T(1024)S(1)} %copy-done.1, bf16[32,8192]{1,0:T(8,128)(2,1)S(1)} %get-tuple-element.4), kind=kLoop, calls=%fused_computation | loop fusion | flops 2097152 | bytes 4227072 | tf_op jit(solution)/shard_map/sub | solution.py:466
Async XLA Ops:
  0.6 106.4 %copy-start = (f32[32,8192]{1,0:T(8,128)S(1)}, f32[32,8192]{1,0:T(8,128)}, u32[]{:S(2)}) copy-start(f32[32,8192]{1,0:T(8,128)} %v_hbm.1) | copy-start | bytes 3145732
  0.6 106.4 %copy-start.1 = (f32[8192]{0:T(1024)S(1)}, f32[8192]{0:T(1024)}, u32[]{:S(2)}) copy-start(f32[8192]{0:T(1024)} %param.5) | copy-start | bytes 98308
